TPU v7x, 32 devices: a whole 2x2x4 slice. The times are simulated.
32 devices in a mesh: seq: 8 (over z, y), head: 4 (over x, core).
Axes of the slice: x: 2, y: 2, z: 4, core: 2. Of those that a mesh axis runs over, the one named last changes fastest.
Arguments:
- queries: bfloat16 [1024, 8, 128], P('seq', 'head'), may hold values from -16 to 16
- values: bfloat16 [1024, 8, 128], P('seq', 'head'), may hold values from -6 to 6
- codes: int32 [8, 1024], P('head', 'seq'), may hold values from 0 to 511, as said below
- codebook: bfloat16 [8, 512, 128], P('head'), may hold values from -0.5 to 0.5
- out_weight: bfloat16 [1024, 2048], P('head'), may hold values from -0.1875 to 0.1875
- grad_out: bfloat16 [1024, 2048], P('seq', 'head'), may hold values from -6 to 6
Outputs:
- grad_queries: bfloat16 [1024, 8, 128], P('seq', 'head')
- grad_values: bfloat16 [1024, 8, 128], P('seq', 'head')
- grad_codebook: float32 [8, 512, 128], P('head')
- grad_weight: bfloat16 [1024, 2048], P('head')
Inputs may be any that keep to these rules, and one draw needn't show every extreme that they name: `codes`: each head's key codeword at each token; both 0 and 511 occur.
All inputs are finite; a program needn't handle non-finite values.
Results may differ from a plain program's by a relative error of at most 0.0065.
Values may be sent and summed in bfloat16 or wider, within the bound.
No kernel may reach another device: no remote copies, remote signals or barrier semaphores. Data moves between devices by JAX's collectives and lax.ppermute only.
A program may use at most 256 MiB of HBM per device.

v0:
```python
import jax
import jax.numpy as jnp
from jax import lax
from jax.sharding import PartitionSpec as P

BLOCK = 128


def entering(value, axis, join, neutral, backward):
    count, mine = (lax.axis_size(axis), lax.axis_index(axis))
    pieces = jax.tree.map(lambda part: lax.all_gather(part, axis), value)
    if backward:
        pieces = jax.tree.map(lambda part: part[::-1], pieces)
        mine = count - 1 - mine
    so_far = jax.tree.map(
        lambda part, zero: jnp.full_like(part, 0) + jnp.asarray(zero, part.dtype), value, neutral
    )

    def turn(position, so_far):
        longer = join(so_far, jax.tree.map(lambda part: part[position], pieces))
        return jax.tree.map(lambda new, old: jnp.where(position < mine, new, old), longer, so_far)

    return lax.fori_loop(0, count - 1, turn, so_far)


def inner_rows(left_side, right_side):
    return lax.dot_general(
        left_side, right_side, (((0,), (0,)), ((), ())), preferred_element_type=jnp.float32
    )


def block_core(query_rows, code_rows, value_rows, grad_rows, cache_sum, cache_count, codebook_head):
    key_rows = jnp.take(codebook_head, code_rows, axis=0)
    contract_last = (((1,), (1,)), ((), ()))
    local_score = lax.dot_general(
        query_rows, key_rows, contract_last, preferred_element_type=jnp.float32
    )
    code_score = lax.dot_general(
        query_rows, codebook_head, contract_last, preferred_element_type=jnp.float32
    )
    length = query_rows.shape[0]
    row_index = lax.broadcasted_iota(jnp.int32, (length, length), 0)
    col_index = lax.broadcasted_iota(jnp.int32, (length, length), 1)
    causal = col_index <= row_index
    top_score = jnp.maximum(
        jnp.max(jnp.where(causal, local_score, -jnp.inf), axis=1), jnp.max(code_score, axis=1)
    )
    weights = jnp.where(causal, jnp.exp(local_score - top_score[:, None]), jnp.float32(0.0))
    cache_weight = jnp.exp(code_score - top_score[:, None])
    denominator = jnp.sum(weights, axis=1) + jnp.sum(cache_weight * cache_count[None, :], axis=1)
    cache_round = cache_sum.astype(jnp.bfloat16)
    numerator = jnp.dot(
        weights.astype(jnp.bfloat16), value_rows, preferred_element_type=jnp.float32
    )
    numerator = numerator + jnp.dot(
        cache_weight.astype(jnp.bfloat16), cache_round, preferred_element_type=jnp.float32
    )
    attended = numerator / denominator[:, None]
    row_delta = jnp.sum(grad_rows.astype(jnp.float32) * attended, axis=1)
    local_grad = lax.dot_general(
        grad_rows, value_rows, contract_last, preferred_element_type=jnp.float32
    )
    cache_grad = lax.dot_general(
        grad_rows, cache_round, contract_last, preferred_element_type=jnp.float32
    )
    grad_local = (weights * (local_grad - row_delta[:, None]) / denominator[:, None]).astype(
        jnp.bfloat16
    )
    grad_cache = (
        cache_weight
        * (cache_grad - row_delta[:, None] * cache_count[None, :])
        / denominator[:, None]
    ).astype(jnp.bfloat16)
    grad_query = jnp.dot(grad_local, key_rows, preferred_element_type=jnp.float32)
    grad_query = (
        grad_query + jnp.dot(grad_cache, codebook_head, preferred_element_type=jnp.float32)
    ).astype(jnp.bfloat16)
    grad_key = inner_rows(grad_local, query_rows)
    key_high = grad_key.astype(jnp.bfloat16)
    key_low = (grad_key - key_high.astype(jnp.float32)).astype(jnp.bfloat16)
    selector = (
        code_rows[:, None] == jnp.arange(codebook_head.shape[0], dtype=jnp.int32)[None, :]
    ).astype(jnp.bfloat16)
    grad_book = inner_rows(selector, key_high) + inner_rows(selector, key_low)
    grad_book = grad_book + inner_rows(grad_cache, query_rows)
    local_share = (weights / denominator[:, None]).astype(jnp.bfloat16)
    cache_share = (cache_weight / denominator[:, None]).astype(jnp.bfloat16)
    grad_value = inner_rows(local_share, grad_rows)
    grad_sum = inner_rows(cache_share, grad_rows)
    return (grad_query, grad_value, grad_sum, grad_book, attended.astype(jnp.bfloat16))


def exclusive_forward(stacked):
    summed = jnp.cumsum(stacked, axis=1)
    return jnp.concatenate([jnp.zeros_like(stacked), summed[:, :-1]], axis=1)


def exclusive_backward(stacked):
    summed = jnp.flip(jnp.cumsum(jnp.flip(stacked, axis=1), axis=1), axis=1)
    return jnp.concatenate([summed[:, 1:], jnp.zeros_like(stacked)], axis=1)


def on_device(queries, values, codes, codebook, out_weight, grad_out):
    tok_here, heads_here, head_width = queries.shape
    code_total = codebook.shape[1]
    blocks = tok_here // BLOCK
    full_grad = lax.all_gather(grad_out, "head", axis=1, tiled=True)
    grad_flat = lax.dot_general(
        full_grad, out_weight, (((1,), (1,)), ((), ())), preferred_element_type=jnp.float32
    ).astype(jnp.bfloat16)
    grad_heads = grad_flat.reshape(tok_here, heads_here, head_width)

    def to_blocks(array):
        return jnp.moveaxis(array.reshape(blocks, BLOCK, heads_here, head_width), 2, 0)

    def from_blocks(array):
        return jnp.moveaxis(array, 0, 2).reshape(tok_here, heads_here, head_width)

    def flatten(array):
        return array.reshape((heads_here * blocks,) + array.shape[2:])

    def unflatten(array):
        return array.reshape((heads_here, blocks) + array.shape[1:])

    code_blocks = codes.reshape(heads_here, blocks, BLOCK)
    query_blocks = to_blocks(queries)
    value_blocks = to_blocks(values)
    grad_blocks = to_blocks(grad_heads)
    selector = (code_blocks[..., None] == jnp.arange(code_total, dtype=jnp.int32)).astype(
        jnp.bfloat16
    )
    block_sums = jnp.einsum(
        "hnbc,hnbd->hncd", selector, value_blocks, preferred_element_type=jnp.float32
    )
    block_counts = jnp.sum(selector, axis=2, dtype=jnp.float32)
    device_parts = (jnp.sum(block_sums, axis=1), jnp.sum(block_counts, axis=1))
    earlier = entering(
        device_parts,
        "seq",
        lambda first_part, second_part: (
            first_part[0] + second_part[0],
            first_part[1] + second_part[1],
        ),
        (jnp.zeros_like(device_parts[0]), jnp.zeros_like(device_parts[1])),
        False,
    )
    cache_sums = earlier[0][:, None] + exclusive_forward(block_sums)
    cache_counts = earlier[1][:, None] + exclusive_forward(block_counts)
    books = jnp.repeat(codebook, blocks, axis=0)
    results = lax.map(
        lambda block_items: block_core(*block_items),
        (
            flatten(query_blocks),
            flatten(code_blocks),
            flatten(value_blocks),
            flatten(grad_blocks),
            flatten(cache_sums),
            flatten(cache_counts),
            books,
        ),
    )
    grad_query = unflatten(results[0])
    grad_value = unflatten(results[1])
    grad_sums = unflatten(results[2])
    grad_books = unflatten(results[3])
    attended = unflatten(results[4])
    device_grad = jnp.sum(grad_sums, axis=1)
    later_grad = entering(
        device_grad,
        "seq",
        lambda first_part, second_part: first_part + second_part,
        jnp.zeros_like(device_grad),
        True,
    )
    carried = later_grad[:, None] + exclusive_backward(grad_sums)
    picked = jax.vmap(jax.vmap(lambda table_rows, indices: jnp.take(table_rows, indices, axis=0)))(
        carried, code_blocks
    )
    grad_values = (grad_value + picked).astype(jnp.bfloat16)
    book_here = jnp.sum(grad_books, axis=1)
    attended_flat = from_blocks(attended).reshape(tok_here, heads_here * head_width)
    weight_term = inner_rows(attended_flat, full_grad)
    summed_weight, summed_book = lax.psum((weight_term, book_here), "seq")
    grad_weight = summed_weight.astype(jnp.bfloat16)
    return (from_blocks(grad_query), from_blocks(grad_values), summed_book, grad_weight)


def solution(mesh):
    return jax.shard_map(
        on_device,
        mesh=mesh,
        in_specs=(
            P("seq", "head", None),
            P("seq", "head", None),
            P("head", "seq"),
            P("head", None, None),
            P("head", None),
            P("seq", "head"),
        ),
        out_specs=(
            P("seq", "head", None),
            P("seq", "head", None),
            P("head", None, None),
            P("head", None),
        ),
        check_vma=False,
    )
```

profile of v0, /device:TPU:0, one launch (start us, length us, event | category | flops | bytes accessed | tf_op | source)
XLA Modules:
  0.0 321.5 jit_solution(7390471878237787274)
XLA Ops:
  7.2 2.0 fusion.71
  9.3 0.9 copy.54
  10.2 8.9 %all_gather.21 = bf16[128,2048]{1,0:T(8,128)(2,1)S(1)} all-gather(bf16[128,512]{1,0:T(8,128)(2,1)} %param.17), channel_id=1, replica_groups=mesh['seq'=8,'head'=4] {'head'}, dimensions={1}, use_global_device_ids=true | all-gather | bytes 655360 | tf_op jit(solution)/shard_map/all_gather | solution.py:107
  19.0 0.5 convolution_convert_fusion
  19.7 0.9 copy.55
  20.5 0.8 convert_reduce_fusion
  21.3 31.5 %all-gather.3 = f32[8,2,512]{2,1,0:T(2,128)S(1)} all-gather(f32[1,2,512]{2,1,0:T(2,128)S(1)} %bitcast.203), channel_id=3, replica_groups=mesh['seq'=8,'head'=4] {'seq'}, dimensions={0}, use_global_device_ids=true | all-gather | bytes 36864 | tf_op jit(solution)/shard_map/all_gather | solution.py:11
  52.9 33.6 %all-gather.7.cloned.1.call-done = f32[16,512,128]{2,1,0:T(8,128)} async-done(((f32[2,512,128]{2,1,0:T(8,128)}), f32[16,512,128]{2,1,0:T(8,128)}) %all-gather.7.cloned.1.call-update) | async-done | bytes 4194320 | tf_op jit(solution)/shard_map/all_gather | solution.py:11
  86.4 8.7 %while.49 = (s32[]{:T(128)}, f32[2,512,128]{2,1,0:T(8,128)S(1)}, f32[2,512]{1,0:T(2,128)S(1)}, s32[]{:T(128)}, f32[8,2,512,128]{3,2,1,0:T(8,128)}, /*index=5*/f32[8,2,512]{2,1,0:T(2,128)S(1)}, s32[]{:T(128)}, s32[]{:T(128)}) while((s32[]{:T(128)}, f32[2,512,128]{2,1,0:T(8,128)S(1)}, f32[2,512]{1,0:T(2,128)S(1)}, s32[]{:T(128)}, ...), condition=%wide.region_2.0_spmd.clone, body=%wide.region_1.0_spmd.clone.sunk | while | flops 396292 | bytes 1585267 | solution.py:23
  86.4 1.2 add_select_fusion.6
  87.7 1.2 add_select_fusion.6
  89.0 1.2 add_select_fusion.6
  90.2 1.2 add_select_fusion.6
  91.5 1.2 add_select_fusion.6
  92.7 1.2 add_select_fusion.6
  94.0 1.2 add_select_fusion.6
  95.2 14.3 %while.48 = (s32[]{:T(128)}, bf16[2,128,128]{2,1,0:T(8,128)(2,1)}, f32[2,128,128]{2,0,1:T(2,128)}, f32[2,512,128]{2,1,0:T(8,128)}, f32[2,512,128]{2,1,0:T(8,128)...) while((s32[]{:T(128)}, bf16[2,128,128]{2,1,0:T(8,128)(2,1)}, ...), condition=%wide.region_9.10_spmd, body=%wide.region_3.9_spmd.sunk | while | flops 161253120 | bytes 12096661 | solution.py:150
  95.4 0.7 gather_fusion
  97.7 0.3 fusion.149
  98.0 0.3 convolution_add_fusion.5
  98.8 0.3 fusion.147
  99.3 0.6 copy-done.4
  99.9 1.4 dynamic_update_slice.31
  102.0 0.4 copy-done.9
  102.5 0.7 gather_fusion
  104.8 0.3 fusion.149
  105.1 0.3 convolution_add_fusion.5
  105.9 0.3 fusion.147
  106.4 0.6 copy-done.4
  107.0 1.4 dynamic_update_slice.31
  109.1 0.4 copy-done.9
  110.0 2.6 fusion.86
  112.6 1.5 copy.53
  114.1 115.8 %all-reduce.4 = bf16[256,2048]{1,0:T(8,128)(2,1)} all-reduce(f32[256,2048]{1,0:T(8,128)} %fusion.86), channel_id=1, replica_groups=mesh['seq'=8,'head'=4] {'seq'}, use_global_device_ids=true, to_apply=%region_13.14 | all-reduce | flops 524288 | bytes 3145728 | tf_op jit(solution)/shard_map/psum | solution.py:183
  230.0 9.5 %all-gather.9.cloned.1.call-done = f32[16,512,128]{2,1,0:T(8,128)} async-done(((f32[2,512,128]{2,1,0:T(8,128)}), f32[16,512,128]{2,1,0:T(8,128)}) %all-gather.9.cloned.1.call-update) | async-done | bytes 4194320 | tf_op jit(solution)/shard_map/all_gather | solution.py:11
  239.5 4.5 %rev.3 = f32[8,2,512,128]{3,2,1,0:T(8,128)} reverse(f32[8,2,512,128]{3,2,1,0:T(8,128)} %bitcast.193), dimensions={0} | reverse | bytes 8388608 | tf_op jit(solution)/shard_map/rev | solution.py:13
  244.0 8.6 %while.50 = (s32[]{:T(128)}, f32[2,512,128]{2,1,0:T(8,128)S(1)}, s32[]{:T(128)}, f32[8,2,512,128]{3,2,1,0:T(8,128)}, s32[]{:T(128)}, /*index=5*/s32[]{:T(128)}) while((s32[]{:T(128)}, f32[2,512,128]{2,1,0:T(8,128)S(1)}, s32[]{:T(128)}, f32[8,2,512,128]{3,2,1,0:T(8,128)}, s32[]{:T(128)}, /*index=5*/s32[]{:T(128)}) %tuple.98), condition=%wide.region_11.12_spmd.clone, body=%wide.region_10.11_spmd.clone.sunk | while | flops 393220 | bytes 1572957 | solution.py:23
  244.0 1.2 add_select_fusion.8
  245.3 1.2 add_select_fusion.8
  246.5 1.2 add_select_fusion.8
  247.7 1.2 add_select_fusion.8
  249.0 1.2 add_select_fusion.8
  250.2 1.2 add_select_fusion.8
  251.4 1.2 add_select_fusion.8
  252.6 1.9 gather_fusion.1
  254.6 0.8 fusion.76
  255.4 57.7 %all-reduce.3.cloned.1.call-done = f32[2,512,128]{2,1,0:T(8,128)} async-done(((f32[2,512,128]{2,1,0:T(8,128)}), f32[2,512,128]{2,1,0:T(8,128)}) %all-reduce.3.cloned.1.call-update) | async-done | bytes 524304 | tf_op jit(solution)/shard_map/psum | solution.py:183
  313.1 1.9 copy.97
  (110 shorter events, 6.5 us)
Async XLA Ops:
  7.2 11.9 %copy-start = (bf16[256,2048]{1,0:T(8,128)(2,1)S(1)}, bf16[256,2048]{1,0:T(8,128)(2,1)}, u32[]{:S(2)}) copy-start(bf16[256,2048]{1,0:T(8,128)(2,1)} %param.16) | copy-start | bytes 3145732
  7.2 79.2 %all-gather.7.cloned.1.call-start = ((), (), s32[]{:S(2)}) async-start(), calls=%async_computation.1 | async-start | bytes 4718592 | tf_op jit(solution)/shard_map/all_gather | solution.py:11
  9.2 230.3 %all-gather.9.cloned.1.call-start = ((), (), s32[]{:S(2)}) async-start(), calls=%async_computation.2 | async-start | bytes 4718592 | tf_op jit(solution)/shard_map/all_gather | solution.py:11
  86.4 8.8 %copy-start.1 = (bf16[2,512,128]{2,1,0:T(8,128)(2,1)S(1)}, bf16[2,512,128]{2,1,0:T(8,128)(2,1)}, u32[]{:S(2)}) copy-start(bf16[2,512,128]{2,1,0:T(8,128)(2,1)} %param.15) | copy-start | bytes 786436
  86.4 8.8 %copy-start.12 = (s32[2,128]{1,0:T(2,128)S(1)}, s32[2,128]{1,0:T(2,128)}, u32[]{:S(2)}) copy-start(s32[2,128]{1,0:T(2,128)} %param.14) | copy-start | bytes 3076
  95.3 4.6 %copy-start.5 = (f32[2,128,128]{2,0,1:T(2,128)S(1)}, f32[2,128,128]{2,0,1:T(2,128)}, u32[]{:S(2)}) copy-start(f32[2,128,128]{2,0,1:T(2,128)} %get-tuple-element.601) | copy-start | bytes 393220 | tf_op jit(solution)/shard_map/while
  95.3 6.3 %copy-start.8 = (bf16[2,128,128]{2,1,0:T(8,128)(2,1)S(1)}, bf16[2,128,128]{2,1,0:T(8,128)(2,1)}, u32[]{:S(2)}) copy-start(bf16[2,128,128]{2,1,0:T(8,128)(2,1)} %get-tuple-element.600) | copy-start | bytes 196612 | tf_op jit(solution)/shard_map/while
  95.3 6.5 %copy-start.10 = (bf16[2,128,128]{1,2,0:T(8,128)(2,1)S(1)}, bf16[2,128,128]{1,2,0:T(8,128)(2,1)}, u32[]{:S(2)}) copy-start(bf16[2,128,128]{1,2,0:T(8,128)(2,1)} %get-tuple-element.604) | copy-start | bytes 196612 | tf_op jit(solution)/shard_map/while
  96.1 2.7 copy-start.3
  99.1 0.8 copy-start.4
  101.3 0.7 copy-start.6
  101.8 0.6 copy-start.9
  101.8 0.6 copy-start.11
  102.4 4.6 %copy-start.5 = (f32[2,128,128]{2,0,1:T(2,128)S(1)}, f32[2,128,128]{2,0,1:T(2,128)}, u32[]{:S(2)}) copy-start(f32[2,128,128]{2,0,1:T(2,128)} %get-tuple-element.601) | copy-start | bytes 393220 | tf_op jit(solution)/shard_map/while
  102.4 6.3 %copy-start.8 = (bf16[2,128,128]{2,1,0:T(8,128)(2,1)S(1)}, bf16[2,128,128]{2,1,0:T(8,128)(2,1)}, u32[]{:S(2)}) copy-start(bf16[2,128,128]{2,1,0:T(8,128)(2,1)} %get-tuple-element.600) | copy-start | bytes 196612 | tf_op jit(solution)/shard_map/while
  102.4 6.5 %copy-start.10 = (bf16[2,128,128]{1,2,0:T(8,128)(2,1)S(1)}, bf16[2,128,128]{1,2,0:T(8,128)(2,1)}, u32[]{:S(2)}) copy-start(bf16[2,128,128]{1,2,0:T(8,128)(2,1)} %get-tuple-element.604) | copy-start | bytes 196612 | tf_op jit(solution)/shard_map/while
  103.2 2.7 copy-start.3
  106.2 0.8 copy-start.4
  108.5 0.7 copy-start.6
  108.9 0.6 copy-start.9
  109.0 0.6 copy-start.11
  109.6 120.3 %copy-start.2 = (f32[2,512,128]{2,1,0:T(8,128)}, f32[2,512,128]{2,1,0:T(8,128)S(1)}, u32[]{:S(2)}) copy-start(f32[2,512,128]{2,1,0:T(8,128)S(1)} %get-tuple-element.270) | copy-start | bytes 1572868
  109.6 203.5 %all-reduce.3.cloned.1.call-start = ((), (), s32[]{:S(2)}) async-start(), calls=%async_computation | async-start | bytes 1048576 | tf_op jit(solution)/shard_map/psum | solution.py:183
  244.0 10.6 %copy-start.7 = (f32[2,128,128]{2,0,1:T(2,128)S(1)}, f32[2,128,128]{2,0,1:T(2,128)}, u32[]{:S(2)}) copy-start(f32[2,128,128]{2,0,1:T(2,128)} %get-tuple-element.267) | copy-start | bytes 393220
Sparse Core Ops, SparseCore 0:
  10.7 75.6 all-gather.6
  109.7 129.6 all-gather.8
  242.9 70.1 all-reduce.2
where the time goes:
time: 323 us; the launch traced here: 322 us
  blocking collectives  156 us (48%)
  waiting for transfers between devices  101 us (31%)
  other arithmetic  19.4 us (6%)
  local copies, waits for them, and re-layouts  18.8 us (6%)
  between operations  13.9 us (4%)
  matrix products  11.5 us (4%)
    psum x1, blocking collectives, on_device(): summed_weight, summed_book = lax.psum((weight_term, book_here), 'seq')  116 us
    psum x1, waiting for transfers between devices, on_device(): summed_weight, summed_book = lax.psum((weight_term, book_here), 'seq')  57.7 us
    all_gather x2, waiting for transfers between devices, entering(): pieces = jax.tree.map(lambda part: lax.all_gather(part, axis), value)  43.1 us
    all_gather x1, blocking collectives, entering(): pieces = jax.tree.map(lambda part: lax.all_gather(part, axis), value)  31.5 us
    select_n x21, other arithmetic, turn(): jnp.where(position < mine, new, old)  17.1 us
    all_gather x1, blocking collectives, on_device(): full_grad = lax.all_gather(grad_out, 'head', axis=1, tiled=True)  8.86 us
  transfers between devices with their start and end apart: 3, of which 3 were waited for; matrix products, arithmetic and copies ran while one was open for 7% of the time, Pallas kernels for 0%

commit v1 on v0

--- a/solution.py
+++ b/solution.py
@@ -104,7 +104,9 @@
     tok_here, heads_here, head_width = queries.shape
     code_total = codebook.shape[1]
     blocks = tok_here // BLOCK
-    full_grad = lax.all_gather(grad_out, "head", axis=1, tiled=True)
+    full_grad = jnp.concatenate(
+        lax.all_to_all(jnp.stack([grad_out] * lax.axis_size("head")), "head", 0, 0), axis=1
+    )
     grad_flat = lax.dot_general(
         full_grad, out_weight, (((1,), (1,)), ((), ())), preferred_element_type=jnp.float32
     ).astype(jnp.bfloat16)

time: 323 us -> 323 us (level)
  blocking collectives: 156 us -> 150 us
  starting transfers between devices: 0.12 us -> 4.32 us
    all_gather x1 -> x0, blocking collectives: 8.86 us -> none  [on_device(): full_grad = lax.all_gather(grad_out, 'head', axis=1, tiled=True)]
    all_to_all x0 -> x1, starting transfers between devices: none -> 4.23 us  [on_device(): lax.all_to_all(jnp.stack([grad_out] * lax.axis_size('head')), 'head', 0, 0)]
  transfers between devices with their start and end apart: 3 -> 4, of which waited for: 3 -> 3; matrix products, arithmetic and copies ran while one was open for 7% -> 8% of each run, Pallas kernels for 0% -> 0%
where the time goes in v1:
time: 323 us; the launch traced here: 321 us
  blocking collectives  150 us (46%)
  waiting for transfers between devices  101 us (31%)
  local copies, waits for them, and re-layouts  20.7 us (6%)
  other arithmetic  19.4 us (6%)
  between operations  13.9 us (4%)
  matrix products  11.5 us (4%)
  starting transfers between devices  4.32 us (1%)
    psum x1, blocking collectives, on_device(): summed_weight, summed_book = lax.psum((weight_term, book_here), 'seq')  118 us
    psum x1, waiting for transfers between devices, on_device(): summed_weight, summed_book = lax.psum((weight_term, book_here), 'seq')  57.5 us
    all_gather x2, waiting for transfers between devices, entering(): pieces = jax.tree.map(lambda part: lax.all_gather(part, axis), value)  43.1 us
    all_gather x1, blocking collectives, entering(): pieces = jax.tree.map(lambda part: lax.all_gather(part, axis), value)  32.3 us
    select_n x21, other arithmetic, turn(): jnp.where(position < mine, new, old)  17 us
  transfers between devices with their start and end apart: 4, of which 3 were waited for; matrix products, arithmetic and copies ran while one was open for 8% of the time, Pallas kernels for 0%

profile of v1, /device:TPU:0, one launch (start us, length us, event | category | flops | bytes accessed | tf_op | source)
XLA Modules:
  0.0 321.5 jit_solution(15033503761919717102)
XLA Ops:
  7.2 2.0 fusion.71
  9.2 1.0 copy.41
  10.2 0.9 stack.2
  11.1 4.2 %all-to-all-start = ((bf16[4,128,512]{1,2,0:T(8,128)(2,1)}), bf16[4,128,512]{1,2,0:T(8,128)(2,1)S(1)}, u32[]{:S(2)}, u32[]{:S(2)}) async-start(bf16[4,128,512]{1,2,0:T(8,128)(2,1)} %stack.2), calls=%async_computation | async-start | bytes 1048576 | tf_op jit(solution)/shard_map/all_to_all | solution.py:108
  15.4 0.9 copy.66
  16.3 0.9 copy.67
  17.1 0.8 convert_reduce_fusion
  17.9 32.3 %all-gather.3 = f32[8,2,512]{2,1,0:T(2,128)S(1)} all-gather(f32[1,2,512]{2,1,0:T(2,128)S(1)} %bitcast.208), channel_id=3, replica_groups=mesh['seq'=8,'head'=4] {'seq'}, dimensions={0}, use_global_device_ids=true | all-gather | bytes 36864 | tf_op jit(solution)/shard_map/all_gather | solution.py:11
  50.3 0.5 convolution_convert_fusion
  50.9 35.0 %all-gather.7.cloned.1.call-done = f32[16,512,128]{2,1,0:T(8,128)} async-done(((f32[2,512,128]{2,1,0:T(8,128)}), f32[16,512,128]{2,1,0:T(8,128)}) %all-gather.7.cloned.1.call-update) | async-done | bytes 4194320 | tf_op jit(solution)/shard_map/all_gather | solution.py:11
  85.9 8.7 %while.49 = (s32[]{:T(128)}, f32[2,512,128]{2,1,0:T(8,128)S(1)}, f32[2,512]{1,0:T(2,128)S(1)}, s32[]{:T(128)}, f32[8,2,512,128]{3,2,1,0:T(8,128)}, /*index=5*/f32[8,2,512]{2,1,0:T(2,128)S(1)}, s32[]{:T(128)}, s32[]{:T(128)}) while((s32[]{:T(128)}, f32[2,512,128]{2,1,0:T(8,128)S(1)}, f32[2,512]{1,0:T(2,128)S(1)}, s32[]{:T(128)}, ...), condition=%wide.region_2.0_spmd.clone, body=%wide.region_1.0_spmd.clone.sunk | while | flops 396292 | bytes 1585267 | solution.py:23
  85.9 1.2 add_select_fusion.6
  87.2 1.2 add_select_fusion.6
  88.4 1.2 add_select_fusion.6
  89.7 1.2 add_select_fusion.6
  90.9 1.2 add_select_fusion.6
  92.2 1.2 add_select_fusion.6
  93.4 1.2 add_select_fusion.6
  94.7 14.3 %while.48 = (s32[]{:T(128)}, bf16[2,128,128]{2,1,0:T(8,128)(2,1)}, f32[2,128,128]{2,0,1:T(2,128)}, f32[2,512,128]{2,1,0:T(8,128)}, f32[2,512,128]{2,1,0:T(8,128)...) while((s32[]{:T(128)}, bf16[2,128,128]{2,1,0:T(8,128)(2,1)}, ...), condition=%wide.region_9.10_spmd, body=%wide.region_3.9_spmd.sunk | while | flops 161253120 | bytes 12096661 | solution.py:152
  94.8 0.7 gather_fusion
  97.1 0.3 fusion.149
  97.5 0.3 convolution_add_fusion.5
  98.7 0.6 copy-done.4
  99.4 1.4 dynamic_update_slice.31
  101.4 0.4 copy-done.9
  102.0 0.7 gather_fusion
  104.3 0.3 fusion.149
  104.6 0.3 convolution_add_fusion.5
  105.9 0.6 copy-done.4
  106.5 1.4 dynamic_update_slice.31
  108.6 0.4 copy-done.9
  109.5 2.6 fusion.86
  112.1 1.5 copy.65
  113.6 118.0 %all-reduce.4 = bf16[256,2048]{1,0:T(8,128)(2,1)} all-reduce(f32[256,2048]{1,0:T(8,128)} %fusion.86), channel_id=1, replica_groups=mesh['seq'=8,'head'=4] {'seq'}, use_global_device_ids=true, to_apply=%region_13.14 | all-reduce | flops 524288 | bytes 3145728 | tf_op jit(solution)/shard_map/psum | solution.py:185
  231.6 8.1 %all-gather.9.cloned.1.call-done = f32[16,512,128]{2,1,0:T(8,128)} async-done(((f32[2,512,128]{2,1,0:T(8,128)}), f32[16,512,128]{2,1,0:T(8,128)}) %all-gather.9.cloned.1.call-update) | async-done | bytes 4194320 | tf_op jit(solution)/shard_map/all_gather | solution.py:11
  239.7 4.5 %rev.3 = f32[8,2,512,128]{3,2,1,0:T(8,128)} reverse(f32[8,2,512,128]{3,2,1,0:T(8,128)} %bitcast.198), dimensions={0} | reverse | bytes 8388608 | tf_op jit(solution)/shard_map/rev | solution.py:13
  244.2 8.6 %while.50 = (s32[]{:T(128)}, f32[2,512,128]{2,1,0:T(8,128)S(1)}, s32[]{:T(128)}, f32[8,2,512,128]{3,2,1,0:T(8,128)}, s32[]{:T(128)}, /*index=5*/s32[]{:T(128)}) while((s32[]{:T(128)}, f32[2,512,128]{2,1,0:T(8,128)S(1)}, s32[]{:T(128)}, f32[8,2,512,128]{3,2,1,0:T(8,128)}, s32[]{:T(128)}, /*index=5*/s32[]{:T(128)}) %tuple.99), condition=%wide.region_11.12_spmd.clone, body=%wide.region_10.11_spmd.clone.sunk | while | flops 393220 | bytes 1572957 | solution.py:23
  244.2 1.2 add_select_fusion.8
  245.4 1.2 add_select_fusion.8
  246.7 1.2 add_select_fusion.8
  247.9 1.2 add_select_fusion.8
  249.1 1.2 add_select_fusion.8
  250.4 1.2 add_select_fusion.8
  251.6 1.2 add_select_fusion.8
  252.8 1.9 gather_fusion.1
  254.7 0.8 fusion.76
  255.6 57.5 %all-reduce.3.cloned.1.call-done = f32[2,512,128]{2,1,0:T(8,128)} async-done(((f32[2,512,128]{2,1,0:T(8,128)}), f32[2,512,128]{2,1,0:T(8,128)}) %all-reduce.3.cloned.1.call-update) | async-done | bytes 524304 | tf_op jit(solution)/shard_map/psum | solution.py:185
  313.1 1.9 copy.109
  (113 shorter events, 7.0 us)
Async XLA Ops:
  7.2 43.1 %copy-start = (bf16[256,2048]{1,0:T(8,128)(2,1)S(1)}, bf16[256,2048]{1,0:T(8,128)(2,1)}, u32[]{:S(2)}) copy-start(bf16[256,2048]{1,0:T(8,128)(2,1)} %param.16) | copy-start | bytes 3145732
  7.2 78.7 %all-gather.7.cloned.1.call-start = ((), (), s32[]{:S(2)}) async-start(), calls=%async_computation.2 | async-start | bytes 4718592 | tf_op jit(solution)/shard_map/all_gather | solution.py:11
  11.1 39.1 %all-to-all-start = ((bf16[4,128,512]{1,2,0:T(8,128)(2,1)}), bf16[4,128,512]{1,2,0:T(8,128)(2,1)S(1)}, u32[]{:S(2)}, u32[]{:S(2)}) async-start(bf16[4,128,512]{1,2,0:T(8,128)(2,1)} %stack.2), calls=%async_computation | async-start | bytes 1048576 | tf_op jit(solution)/shard_map/all_to_all | solution.py:108
  15.3 224.3 %all-gather.9.cloned.1.call-start = ((), (), s32[]{:S(2)}) async-start(), calls=%async_computation.3 | async-start | bytes 4718592 | tf_op jit(solution)/shard_map/all_gather | solution.py:11
  85.9 8.8 %copy-start.1 = (bf16[2,512,128]{2,1,0:T(8,128)(2,1)S(1)}, bf16[2,512,128]{2,1,0:T(8,128)(2,1)}, u32[]{:S(2)}) copy-start(bf16[2,512,128]{2,1,0:T(8,128)(2,1)} %param.15) | copy-start | bytes 786436
  85.9 8.8 %copy-start.12 = (s32[2,128]{1,0:T(2,128)S(1)}, s32[2,128]{1,0:T(2,128)}, u32[]{:S(2)}) copy-start(s32[2,128]{1,0:T(2,128)} %param.14) | copy-start | bytes 3076
  94.7 4.6 %copy-start.5 = (f32[2,128,128]{2,0,1:T(2,128)S(1)}, f32[2,128,128]{2,0,1:T(2,128)}, u32[]{:S(2)}) copy-start(f32[2,128,128]{2,0,1:T(2,128)} %get-tuple-element.614) | copy-start | bytes 393220 | tf_op jit(solution)/shard_map/while
  94.7 6.3 %copy-start.8 = (bf16[2,128,128]{2,1,0:T(8,128)(2,1)S(1)}, bf16[2,128,128]{2,1,0:T(8,128)(2,1)}, u32[]{:S(2)}) copy-start(bf16[2,128,128]{2,1,0:T(8,128)(2,1)} %get-tuple-element.613) | copy-start | bytes 196612 | tf_op jit(solution)/shard_map/while
  94.7 6.5 %copy-start.10 = (bf16[2,128,128]{1,2,0:T(8,128)(2,1)S(1)}, bf16[2,128,128]{1,2,0:T(8,128)(2,1)}, u32[]{:S(2)}) copy-start(bf16[2,128,128]{1,2,0:T(8,128)(2,1)} %get-tuple-element.617) | copy-start | bytes 196612 | tf_op jit(solution)/shard_map/while
  95.5 2.7 copy-start.3
  98.6 0.8 copy-start.4
  100.8 0.6 copy-start.6
  101.2 0.6 copy-start.9
  101.3 0.6 copy-start.11
  101.9 4.6 %copy-start.5 = (f32[2,128,128]{2,0,1:T(2,128)S(1)}, f32[2,128,128]{2,0,1:T(2,128)}, u32[]{:S(2)}) copy-start(f32[2,128,128]{2,0,1:T(2,128)} %get-tuple-element.614) | copy-start | bytes 393220 | tf_op jit(solution)/shard_map/while
  101.9 6.3 %copy-start.8 = (bf16[2,128,128]{2,1,0:T(8,128)(2,1)S(1)}, bf16[2,128,128]{2,1,0:T(8,128)(2,1)}, u32[]{:S(2)}) copy-start(bf16[2,128,128]{2,1,0:T(8,128)(2,1)} %get-tuple-element.613) | copy-start | bytes 196612 | tf_op jit(solution)/shard_map/while
  101.9 6.5 %copy-start.10 = (bf16[2,128,128]{1,2,0:T(8,128)(2,1)S(1)}, bf16[2,128,128]{1,2,0:T(8,128)(2,1)}, u32[]{:S(2)}) copy-start(bf16[2,128,128]{1,2,0:T(8,128)(2,1)} %get-tuple-element.617) | copy-start | bytes 196612 | tf_op jit(solution)/shard_map/while
  102.7 2.7 copy-start.3
  105.7 0.8 copy-start.4
  107.9 0.6 copy-start.6
  108.4 0.6 copy-start.9
  108.4 0.6 copy-start.11
  109.0 122.5 %copy-start.2 = (f32[2,512,128]{2,1,0:T(8,128)}, f32[2,512,128]{2,1,0:T(8,128)S(1)}, u32[]{:S(2)}) copy-start(f32[2,512,128]{2,1,0:T(8,128)S(1)} %get-tuple-element.270) | copy-start | bytes 1572868
  109.1 204.0 %all-reduce.3.cloned.1.call-start = ((), (), s32[]{:S(2)}) async-start(), calls=%async_computation.1 | async-start | bytes 1048576 | tf_op jit(solution)/shard_map/psum | solution.py:185
  244.2 10.5 %copy-start.7 = (f32[2,128,128]{2,0,1:T(2,128)S(1)}, f32[2,128,128]{2,0,1:T(2,128)}, u32[]{:S(2)}) copy-start(f32[2,128,128]{2,0,1:T(2,128)} %get-tuple-element.267) | copy-start | bytes 393220
Sparse Core Ops, SparseCore 0:
  10.1 75.7 all-gather.6
  109.2 130.4 all-gather.8
  243.1 69.9 all-reduce.2
